TPU v7x, 32 devices: a whole 2x2x4 slice. The times are simulated.
32 devices in a mesh: lat: 4 (over y, x), lon: 8 (over z, core).
Axes of the slice: x: 2, y: 2, z: 4, core: 2. Of those that a mesh axis runs over, the one named last changes fastest.
Arguments:
- signal: bfloat16 [96, 144, 512], P('lat', 'lon'), may hold values from -6 to 6
- band_rows: int32 [4], replicated, may hold values from 12 to 24, as said below
- support_rows: int32 [72, 16], replicated, may hold values from 0 to 71, as said below
- support_lons: int32 [72, 16], replicated, may hold values from 0 to 143, as said below
- basis_values: bfloat16 [72, 16, 9], replicated, may hold values from -1.5 to 1.5
- mixing: bfloat16 [9, 512, 512], P(None, 'lon'), may hold values from -0.09375 to 0.09375
Outputs:
- convolved: bfloat16 [96, 144, 512], P('lat', 'lon')
Inputs may be any that keep to these rules, and one draw needn't show every extreme that they name: `band_rows`: the counts sum to 72; the largest is 24. `support_rows`: every entry of grid row i lies within 2 rows of i. `support_lons`: for rows i with 2 <= i < 70, each offset is at most 2 or at least 142; rows nearer a pole may take any offset.
All inputs are finite; a program needn't handle non-finite values.
Results may differ from a plain program's by a relative error of at most 0.0049.
Values may be sent and summed in bfloat16 or wider, within the bound.
A program may use at most 64 MiB of HBM per device.

v0:
```python
import jax
import jax.numpy as jnp
from jax import lax
from jax.sharding import PartitionSpec as P

LAT_REACH = 2
LON_REACH = 2
POLAR_ROWS = 2


def extended_2(block, sides, width, periodic):
    for axis, dim in sides:
        count = lax.axis_size(axis)
        forward = [(i, i + 1) for i in range(count - 1)]
        if periodic:
            forward.append((count - 1, 0))
        backward = [(target, source) for source, target in forward]
        low = lax.ppermute(
            lax.slice_in_dim(block, block.shape[dim] - width, None, axis=dim), axis, forward
        )
        high = lax.ppermute(lax.slice_in_dim(block, 0, width, axis=dim), axis, backward)
        block = jnp.concatenate([low, block, high], axis=dim)
    return block


def signed_offset(offset, cycle_len):
    return jnp.where(offset > cycle_len // 2, offset - cycle_len, offset)


def contract_rows(table_basis, pieces):
    flattened = pieces.reshape(pieces.shape[0], -1)
    summed = jnp.dot(table_basis.T, flattened, preferred_element_type=jnp.float32)
    return summed.astype(jnp.bfloat16).reshape((table_basis.shape[1],) + pieces.shape[1:])


def per_device(signal, band_rows, support_rows, support_lons, basis_values, mixing):
    band_index = lax.axis_index("lat")
    lon_index = lax.axis_index("lon")
    band_total = lax.axis_size("lat")
    cycle_total = lax.axis_size("lon")
    rows_dev, lon_dev, channels = signal.shape
    cycle_len = lon_dev * cycle_total
    grid_rows = support_rows.shape[0]
    starts = jnp.cumsum(band_rows) - band_rows
    live_rows = band_rows[band_index]
    first_row = starts[band_index]
    is_bottom = band_index == band_total - 1
    has_polar = (band_index == 0) | is_bottom
    polar_span = POLAR_ROWS + LAT_REACH
    upper_rim = signal[:LAT_REACH]
    lower_rim = lax.dynamic_slice_in_dim(signal, live_rows - LAT_REACH, LAT_REACH, 0)
    edge_rows = jnp.concatenate([upper_rim, lower_rim], 0)
    rim_rows = extended_2(edge_rows, (("lat", 0),), LAT_REACH, False)
    extended = jnp.concatenate([rim_rows[:LAT_REACH], signal, jnp.zeros_like(upper_rim)], 0)
    extended = lax.dynamic_update_slice_in_dim(
        extended, rim_rows[3 * LAT_REACH :], LAT_REACH + live_rows, 0
    )
    cycle_cells = extended_2(extended, (("lon", 1),), LON_REACH, True)
    polar_start = jnp.where(is_bottom, live_rows - polar_span, 0)
    polar_source = lax.dynamic_slice_in_dim(signal, polar_start, polar_span, 0)
    source_base = jnp.where(is_bottom, grid_rows - polar_span, 0)
    output_base = jnp.where(is_bottom, grid_rows - POLAR_ROWS, 0)
    polar_ids = jnp.clip(output_base + jnp.arange(POLAR_ROWS), 0, grid_rows - 1)
    polar_src = support_rows[polar_ids] - source_base
    polar_off = support_lons[polar_ids]
    polar_basis = basis_values[polar_ids]
    whole_cycle = lax.all_gather(polar_source, "lon", axis=1, tiled=True)
    wrapped = jnp.concatenate([whole_cycle, whole_cycle[:, :lon_dev]], 1)
    col_starts = (lon_index * lon_dev + polar_off) % cycle_len

    def cycle_piece(row_id, col_id):
        return lax.dynamic_slice(wrapped, (row_id, col_id, 0), (1, lon_dev, channels))[0]

    polar_pieces = jax.vmap(jax.vmap(cycle_piece))(polar_src, col_starts)
    polar_z = jax.vmap(contract_rows)(polar_basis, polar_pieces)
    full_mixing = lax.all_gather(mixing, "lon", axis=1, tiled=True)
    polar_slot = jnp.where(is_bottom, live_rows - POLAR_ROWS, 0)

    def row_terms(slot_id):
        grid_id = jnp.clip(first_row + slot_id, 0, grid_rows - 1)
        local_rows = support_rows[grid_id] - first_row + LAT_REACH
        local_cols = signed_offset(support_lons[grid_id], cycle_len) + LON_REACH

        def band_piece(row_id, col_id):
            return lax.dynamic_slice(cycle_cells, (row_id, col_id, 0), (1, lon_dev, channels))[0]

        pieces = jax.vmap(band_piece)(local_rows, local_cols)
        banded = contract_rows(basis_values[grid_id], pieces)
        polar_pos = slot_id - polar_slot
        use_polar = has_polar & (polar_pos >= 0) & (polar_pos < POLAR_ROWS)
        chosen = polar_z[jnp.clip(polar_pos, 0, POLAR_ROWS - 1)]
        return jnp.where(use_polar, chosen, banded)

    block_rows = 8

    def block_out(block_id):
        slot_ids = block_id * block_rows + jnp.arange(block_rows)
        basis_terms = jax.vmap(row_terms)(slot_ids)
        mixed_block = jnp.einsum(
            "rklc,kco->rlo", basis_terms, full_mixing, preferred_element_type=jnp.float32
        )
        keep_rows = (slot_ids < live_rows)[:, None, None]
        return jnp.where(keep_rows, mixed_block, 0.0).astype(jnp.bfloat16)

    blocks = lax.map(block_out, jnp.arange(rows_dev // block_rows))
    return blocks.reshape(rows_dev, lon_dev, full_mixing.shape[2])


def solution(mesh):
    placed = (P("lat", "lon", None), P(), P(), P(), P(), P(None, "lon", None))
    return jax.shard_map(
        per_device, mesh=mesh, in_specs=placed, out_specs=P("lat", "lon", None), check_vma=False
    )
```

profile of v0, /device:TPU:0, one launch (start us, length us, event | category | flops | bytes accessed | tf_op | source)
XLA Modules:
  0.0 169.7 jit_solution(472577886050172118)
XLA Ops:
  6.5 0.7 all-gather.2.cloned.1.call-update
  7.3 1.3 dynamic_slice.19
  9.8 1.1 fusion.34
  10.9 4.8 %collective-permute-start = (bf16[2,18,512]{2,0,1:T(2,128)(2,1)S(1)}, bf16[2,18,512]{2,0,1:T(2,128)(2,1)S(1)}, u32[]{:S(2)}, u32[]{:S(2)}) collective-permute-start(bf16[2,18,512]{2,0,1:T(2,128)(2,1)S(1)} %get-tuple-element.241), channel_id=1, source_target_pairs={{0,8},{8,16},{16,24},{1,9},{9,17},{17,25},{2,10},{10,18},{18,26},{... | collective-permute-start | bytes 110600 | tf_op jit(solution)/shard_map/ppermute | solution.py:18
  15.8 1.3 collective-permute-start.1
  17.7 1.0 constant_dynamic-slice_fusion.1
  18.8 18.6 %all_gather.6 = bf16[4,144,512]{2,0,1:T(4,128)(2,1)S(1)} all-gather(bf16[4,18,512]{2,0,1:T(4,128)(2,1)S(1)} %constant_dynamic-slice_fusion.1), channel_id=1, replica_groups=mesh['lat'=4,'lon'=8] {'lon'}, dimensions={1}, use_global_device_ids=true | all-gather | bytes 663552 | tf_op jit(solution)/shard_map/all_gather | solution.py:67
  37.4 1.4 copy.32
  38.8 0.7 copy.33
  39.5 1.3 gather_fusion.6
  40.9 1.3 gather_fusion.7
  42.7 2.3 %gather_fusion.8 = bf16[32,18,512]{2,0,1:T(8,128)(2,1)S(1)} fusion(bf16[4,162,512]{2,0,1:T(4,128)(2,1)S(1)} %pad_maximum_fusion.1, s32[32]{0:T(128)S(1)} %reshape.300), kind=kCustom, calls=%fused_computation.8 | custom fusion | bytes 1180032 | tf_op jit(solution)/shard_map/vmap(vmap())/gather | solution.py:72
  48.9 2.0 %dynamic_update_slice.10 = bf16[28,18,512]{2,0,1:T(8,128)(2,1)S(1)} dynamic-update-slice(bf16[28,18,512]{2,0,1:T(8,128)(2,1)S(1)} %maximum_maximum_fusion, bf16[2,18,512]{2,0,1:T(2,128)(2,1)S(1)} %collective-permute-done.1, s32[]{:T(128)S(6)} %select_n.166, s32[]{:T(128)} %copy.75, s32[]{:T(128)} %copy.75) | dynamic-update-slice | bytes 73732 | tf_op jit(solution)/shard_map/dynamic_update_slice | solution.py:55
  51.3 3.2 %collective-permute-start.3 = (bf16[28,2,512]{2,0,1:T(8,128)(2,1)S(1)}, bf16[28,2,512]{2,0,1:T(8,128)(2,1)S(1)}, u32[]{:S(2)}, u32[]{:S(2)}) collective-permute-start(bf16[28,2,512]{2,0,1:T(8,128)(2,1)S(1)} %get-tuple-element.239), channel_id=1, source_target_pairs={{1,0},{2,1},{3,2},{4,3},{5,4},{6,5},{7,6},{0,7},{9,8},{10,9},{11,1... | collective-permute-start | bytes 172040 | tf_op jit(solution)/shard_map/ppermute | solution.py:21
  54.5 1.0 copy.38
  56.4 1.8 %collective-permute-done.2 = bf16[28,2,512]{2,0,1:T(8,128)(2,1)S(1)} collective-permute-done((bf16[28,2,512]{2,0,1:T(8,128)(2,1)S(1)}, bf16[28,2,512]{2,0,1:T(8,128)(2,1)S(1)}, u32[]{:S(2)}, u32[]{:S(2)}) %collective-permute-start.2) | collective-permute-done | bytes 57376 | tf_op jit(solution)/shard_map/ppermute | solution.py:18
  58.3 11.0 %all-gather.2.cloned.1.call-done = bf16[9,512,512]{2,1,0:T(8,128)(2,1)} async-done(((bf16[9,64,512]{2,1,0:T(8,128)(2,1)}), bf16[9,512,512]{2,1,0:T(8,128)(2,1)}) %all-gather.2.cloned.1.call-update) | async-done | bytes 4718608 | tf_op jit(solution)/shard_map/all_gather | solution.py:76
  69.3 93.5 %while.12 = (s32[]{:T(128)}, bf16[3,8,18,512]{3,1,0,2:T(8,128)(2,1)}, s32[3]{0:T(128)S(1)}, s32[]{:T(128)}, pred[]{:T(512)}, /*index=5*/s32[]{:T(128)}, bf16[2,9...) while((s32[]{:T(128)}, ...), condition=%wide.region_2.3_spmd, body=%wide.region_1.2_spmd.sunk | while | flops 702187840 | bytes 30979968 | solution.py:105
  71.2 1.4 gather_fusion.2
  72.6 1.3 gather_fusion.3
  74.6 7.8 %gather_fusion.4 = bf16[128,18,512]{2,0,1:T(8,128)(2,1)S(1)} fusion(bf16[28,22,512]{2,0,1:T(8,128)(2,1)S(1)} %get-tuple-element.370, s32[128]{0:T(128)S(1)} %reshape.345), kind=kCustom, calls=%fused_computation.4.clone.1 | custom fusion | bytes 4720128 | tf_op jit(solution)/shard_map/while/body/eval_jaxpr/vmap(vmap())/gather | solution.py:85
  82.4 3.0 %copy.64 = bf16[128,18,512]{2,1,0:T(8,128)(2,1)} copy(bf16[128,18,512]{2,0,1:T(8,128)(2,1)S(1)} %gather_fusion.4) | data formatting | bytes 4718592 | tf_op jit(solution)/shard_map/while/body/eval_jaxpr/vmap(vmap())/gather | solution.py:85
  85.4 3.3 %squeeze.40 = bf16[8,16,9216]{2,1,0:T(8,128)(2,1)S(1)} reshape(bf16[128,18,512]{2,1,0:T(8,128)(2,1)} %copy.64) | data formatting | bytes 4718592 | tf_op jit(solution)/shard_map/while/body/eval_jaxpr/vmap()/reshape;while/body/eval_jaxpr/vmap(vmap())/squeeze | solution.py:31
  88.8 2.1 %gather_fusion.1 = bf16[8,16,9]{1,2,0:T(8,128)(2,1)} fusion(bf16[72,16,9]{1,2,0:T(8,128)(2,1)} %get-tuple-element.367, s32[8]{0:T(128)S(1)} %get-tuple-element.326), kind=kCustom, calls=%fused_computation.1.clone.1 | custom fusion | bytes 4704 | tf_op jit(solution)/shard_map/while/body/eval_jaxpr/vmap()/gather | solution.py:88
  90.9 1.5 convolution_convert_fusion.3
  92.4 1.9 %copy.65 = bf16[8,9,9216]{2,0,1:T(8,128)(2,1)} copy(bf16[8,9,9216]{2,1,0:T(8,128)(2,1)S(1)} %convolution_convert_fusion.3) | data formatting | bytes 2654208 | tf_op jit(solution)/shard_map/while/body/eval_jaxpr/vmap()/convert_element_type | solution.py:33
  95.6 4.1 %fusion.50 = bf16[1,8,18,512]{3,2,1,0:T(8,128)(2,1)S(1)} fusion(bf16[9,512,512]{2,1,0:T(8,128)(2,1)} %get-tuple-element.371, bf16[8,9,18,512]{3,2,1,0:T(8,128)(2,1)S(1)} %gather_fusion, bf16[8,9,18,512]{3,0,2,1:T(8,128)(2,1)} %bitcast.78, pred[8]{0:T(512)(128)(4,1)S(1)} %get-tuple-element.327, pred[8]{0:T(512)(128)(4,1)S(1)} %get-tuple-element.328), kind=kOutput, calls=%fused_computation.17.clone.1 | convolution fusion | flops 680288256 | bytes 7520272 | tf_op jit(solution)/shard_map/while/body/eval_jaxpr/rklc,kco->rlo/dot_general | solution.py:99
  99.8 0.7 copy_dynamic-update-slice_fusion.2
  102.4 1.4 gather_fusion.2
  103.7 1.4 gather_fusion.3
  105.8 7.8 %gather_fusion.4 = bf16[128,18,512]{2,0,1:T(8,128)(2,1)S(1)} fusion(bf16[28,22,512]{2,0,1:T(8,128)(2,1)S(1)} %get-tuple-element.370, s32[128]{0:T(128)S(1)} %reshape.345), kind=kCustom, calls=%fused_computation.4.clone.1 | custom fusion | bytes 4720128 | tf_op jit(solution)/shard_map/while/body/eval_jaxpr/vmap(vmap())/gather | solution.py:85
  113.6 3.0 %copy.64 = bf16[128,18,512]{2,1,0:T(8,128)(2,1)} copy(bf16[128,18,512]{2,0,1:T(8,128)(2,1)S(1)} %gather_fusion.4) | data formatting | bytes 4718592 | tf_op jit(solution)/shard_map/while/body/eval_jaxpr/vmap(vmap())/gather | solution.py:85
  116.6 3.3 %squeeze.40 = bf16[8,16,9216]{2,1,0:T(8,128)(2,1)S(1)} reshape(bf16[128,18,512]{2,1,0:T(8,128)(2,1)} %copy.64) | data formatting | bytes 4718592 | tf_op jit(solution)/shard_map/while/body/eval_jaxpr/vmap()/reshape;while/body/eval_jaxpr/vmap(vmap())/squeeze | solution.py:31
  119.9 2.1 %gather_fusion.1 = bf16[8,16,9]{1,2,0:T(8,128)(2,1)} fusion(bf16[72,16,9]{1,2,0:T(8,128)(2,1)} %get-tuple-element.367, s32[8]{0:T(128)S(1)} %get-tuple-element.326), kind=kCustom, calls=%fused_computation.1.clone.1 | custom fusion | bytes 4704 | tf_op jit(solution)/shard_map/while/body/eval_jaxpr/vmap()/gather | solution.py:88
  122.1 1.5 convolution_convert_fusion.3
  123.6 1.9 %copy.65 = bf16[8,9,9216]{2,0,1:T(8,128)(2,1)} copy(bf16[8,9,9216]{2,1,0:T(8,128)(2,1)S(1)} %convolution_convert_fusion.3) | data formatting | bytes 2654208 | tf_op jit(solution)/shard_map/while/body/eval_jaxpr/vmap()/convert_element_type | solution.py:33
  126.8 4.1 %fusion.50 = bf16[1,8,18,512]{3,2,1,0:T(8,128)(2,1)S(1)} fusion(bf16[9,512,512]{2,1,0:T(8,128)(2,1)} %get-tuple-element.371, bf16[8,9,18,512]{3,2,1,0:T(8,128)(2,1)S(1)} %gather_fusion, bf16[8,9,18,512]{3,0,2,1:T(8,128)(2,1)} %bitcast.78, pred[8]{0:T(512)(128)(4,1)S(1)} %get-tuple-element.327, pred[8]{0:T(512)(128)(4,1)S(1)} %get-tuple-element.328), kind=kOutput, calls=%fused_computation.17.clone.1 | convolution fusion | flops 680288256 | bytes 7520272 | tf_op jit(solution)/shard_map/while/body/eval_jaxpr/rklc,kco->rlo/dot_general | solution.py:99
  130.9 0.7 copy_dynamic-update-slice_fusion.2
  133.6 1.4 gather_fusion.2
  134.9 1.3 gather_fusion.3
  137.0 7.8 %gather_fusion.4 = bf16[128,18,512]{2,0,1:T(8,128)(2,1)S(1)} fusion(bf16[28,22,512]{2,0,1:T(8,128)(2,1)S(1)} %get-tuple-element.370, s32[128]{0:T(128)S(1)} %reshape.345), kind=kCustom, calls=%fused_computation.4.clone.1 | custom fusion | bytes 4720128 | tf_op jit(solution)/shard_map/while/body/eval_jaxpr/vmap(vmap())/gather | solution.py:85
  144.7 3.0 %copy.64 = bf16[128,18,512]{2,1,0:T(8,128)(2,1)} copy(bf16[128,18,512]{2,0,1:T(8,128)(2,1)S(1)} %gather_fusion.4) | data formatting | bytes 4718592 | tf_op jit(solution)/shard_map/while/body/eval_jaxpr/vmap(vmap())/gather | solution.py:85
  147.8 3.3 %squeeze.40 = bf16[8,16,9216]{2,1,0:T(8,128)(2,1)S(1)} reshape(bf16[128,18,512]{2,1,0:T(8,128)(2,1)} %copy.64) | data formatting | bytes 4718592 | tf_op jit(solution)/shard_map/while/body/eval_jaxpr/vmap()/reshape;while/body/eval_jaxpr/vmap(vmap())/squeeze | solution.py:31
  151.1 2.1 %gather_fusion.1 = bf16[8,16,9]{1,2,0:T(8,128)(2,1)} fusion(bf16[72,16,9]{1,2,0:T(8,128)(2,1)} %get-tuple-element.367, s32[8]{0:T(128)S(1)} %get-tuple-element.326), kind=kCustom, calls=%fused_computation.1.clone.1 | custom fusion | bytes 4704 | tf_op jit(solution)/shard_map/while/body/eval_jaxpr/vmap()/gather | solution.py:88
  153.2 1.5 convolution_convert_fusion.3
  154.7 1.9 %copy.65 = bf16[8,9,9216]{2,0,1:T(8,128)(2,1)} copy(bf16[8,9,9216]{2,1,0:T(8,128)(2,1)S(1)} %convolution_convert_fusion.3) | data formatting | bytes 2654208 | tf_op jit(solution)/shard_map/while/body/eval_jaxpr/vmap()/convert_element_type | solution.py:33
  158.0 4.1 %fusion.50 = bf16[1,8,18,512]{3,2,1,0:T(8,128)(2,1)S(1)} fusion(bf16[9,512,512]{2,1,0:T(8,128)(2,1)} %get-tuple-element.371, bf16[8,9,18,512]{3,2,1,0:T(8,128)(2,1)S(1)} %gather_fusion, bf16[8,9,18,512]{3,0,2,1:T(8,128)(2,1)} %bitcast.78, pred[8]{0:T(512)(128)(4,1)S(1)} %get-tuple-element.327, pred[8]{0:T(512)(128)(4,1)S(1)} %get-tuple-element.328), kind=kOutput, calls=%fused_computation.17.clone.1 | convolution fusion | flops 680288256 | bytes 7520272 | tf_op jit(solution)/shard_map/while/body/eval_jaxpr/rklc,kco->rlo/dot_general | solution.py:99
  162.1 0.7 copy_dynamic-update-slice_fusion.2
  (53 shorter events, 14.3 us)
Async XLA Ops:
  6.5 32.3 %copy-start.2 = (s32[72,16]{0,1:T(8,128)S(1)}, s32[72,16]{0,1:T(8,128)}, u32[]{:S(2)}) copy-start(s32[72,16]{0,1:T(8,128)} %param.11) | copy-start | bytes 13828
  6.5 62.8 %all-gather.2.cloned.1.call-start = ((), (), s32[]{:S(2)}) async-start(), calls=%async_computation | async-start | bytes 5308416 | tf_op jit(solution)/shard_map/all_gather | solution.py:76
  10.9 37.7 %collective-permute-start = (bf16[2,18,512]{2,0,1:T(2,128)(2,1)S(1)}, bf16[2,18,512]{2,0,1:T(2,128)(2,1)S(1)}, u32[]{:S(2)}, u32[]{:S(2)}) collective-permute-start(bf16[2,18,512]{2,0,1:T(2,128)(2,1)S(1)} %get-tuple-element.241), channel_id=1, source_target_pairs={{0,8},{8,16},{16,24},{1,9},{9,17},{17,25},{2,10},{10,18},{18,26},{... | collective-permute-start | bytes 110600 | tf_op jit(solution)/shard_map/ppermute | solution.py:18
  15.8 33.2 %collective-permute-start.1 = (bf16[2,18,512]{2,0,1:T(2,128)(2,1)S(1)}, bf16[2,18,512]{2,0,1:T(2,128)(2,1)S(1)}, u32[]{:S(2)}, u32[]{:S(2)}) collective-permute-start(bf16[2,18,512]{2,0,1:T(2,128)(2,1)S(1)} %get-tuple-element.240), channel_id=1, source_target_pairs={{8,0},{16,8},{24,16},{9,1},{17,9},{25,17},{10,2},{18,10},{26,18},{... | collective-permute-start | bytes 110600 | tf_op jit(solution)/shard_map/ppermute | solution.py:21
  45.1 0.8 copy-start.1
  45.4 2.9 %copy-start.3 = (s32[4]{0:T(128)S(1)}, s32[4]{0:T(128)}, u32[]{:S(2)}) copy-start(s32[4]{0:T(128)} %param.9) | copy-start | bytes 52
  45.4 3.2 %copy-start = (bf16[24,18,512]{2,0,1:T(8,128)(2,1)S(1)}, bf16[24,18,512]{2,0,1:T(8,128)(2,1)}, u32[]{:S(2)}) copy-start(bf16[24,18,512]{2,0,1:T(8,128)(2,1)} %param.8) | copy-start | bytes 1327108
  50.9 7.3 %collective-permute-start.2 = (bf16[28,2,512]{2,0,1:T(8,128)(2,1)S(1)}, bf16[28,2,512]{2,0,1:T(8,128)(2,1)S(1)}, u32[]{:S(2)}, u32[]{:S(2)}) collective-permute-start(bf16[28,2,512]{2,0,1:T(8,128)(2,1)S(1)} %get-tuple-element.238), channel_id=1, source_target_pairs={{0,1},{1,2},{2,3},{3,4},{4,5},{5,6},{6,7},{7,0},{8,9},{9,10},{10,1... | collective-permute-start | bytes 172040 | tf_op jit(solution)/shard_map/ppermute | solution.py:18
  51.3 6.9 %collective-permute-start.3 = (bf16[28,2,512]{2,0,1:T(8,128)(2,1)S(1)}, bf16[28,2,512]{2,0,1:T(8,128)(2,1)S(1)}, u32[]{:S(2)}, u32[]{:S(2)}) collective-permute-start(bf16[28,2,512]{2,0,1:T(8,128)(2,1)S(1)} %get-tuple-element.239), channel_id=1, source_target_pairs={{1,0},{2,1},{3,2},{4,3},{5,4},{6,5},{7,6},{0,7},{9,8},{10,9},{11,1... | collective-permute-start | bytes 172040 | tf_op jit(solution)/shard_map/ppermute | solution.py:21
Sparse Core Ops, SparseCore 0:
  8.9 60.3 all-gather.1
where the time goes:
time: 171 us; the launch traced here: 170 us
  local copies, waits for them, and re-layouts  85 us (50%)
  blocking collectives  18.6 us (11%)
  matrix products  17.3 us (10%)
  between operations  16.7 us (10%)
  waiting for transfers between devices  13.6 us (8%)
  starting transfers between devices  9.7 us (6%)
  other arithmetic  6.76 us (4%)
  loops' own time  2.05 us (1%)
    gather x6, local copies, waits for them, and re-layouts, band_piece(): lax.dynamic_slice(cycle_cells, (row_id, col_id, 0), (1, lon_dev, channels))  32.3 us
    all_gather x1, blocking collectives, per_device(): whole_cycle = lax.all_gather(polar_source, 'lon', axis=1, tiled=True)  18.6 us
    dot_general x3, matrix products, block_out(): jnp.einsum('rklc,kco->rlo', basis_terms, full_mixing, preferred_element_t...  12.4 us
    all_gather x1, waiting for transfers between devices, per_device(): full_mixing = lax.all_gather(mixing, 'lon', axis=1, tiled=True)  11 us
    squeeze x4, local copies, waits for them, and re-layouts, contract_rows(): flattened = pieces.reshape(pieces.shape[0], -1)  10.3 us
    gather x3, local copies, waits for them, and re-layouts, row_terms(): banded = contract_rows(basis_values[grid_id], pieces)  6.43 us
    convert_element_type x3, local copies, waits for them, and re-layouts, contract_rows(): summed.astype(jnp.bfloat16)  5.7 us
    ppermute x2, starting transfers between devices, extended_2(): lax.ppermute(lax.slice_in_dim(block, block.shape[dim] - width, None, axis...  5.21 us
  transfers between devices with their start and end apart: 5, of which 2 were waited for; matrix products, arithmetic and copies ran while one was open for 10% of the time, Pallas kernels for 0%

commit v1 on v0

v1 whole, which is shorter than its diff:
```python
import functools

import jax
import jax.numpy as jnp
from jax import lax
from jax.experimental import pallas as pl
from jax.experimental.pallas import tpu as pltpu
from jax.sharding import PartitionSpec as P

LAT_REACH = 2
LON_REACH = 2
POLAR_ROWS = 2
SPAN = POLAR_ROWS + LAT_REACH
GROUP = 4
PAD = 24
WIDE = 32
PIECES = 4
CHUNKS = 3
POLAR_PAD = 80
MESH = pl.DeviceIdType.MESH
BF16 = jnp.bfloat16
F32 = jnp.float32


def rdma(src, dst, send_sem, recv_sem, lat, lon):
    return pltpu.make_async_remote_copy(
        src_ref=src, dst_ref=dst, send_sem=send_sem, recv_sem=recv_sem,
        device_id=(lat, lon), device_id_type=MESH,
    )


def kernel(
    n_lat, n_lon, grid_rows,
    signal, band_rows, sup_rows, sup_lons, basis, mixing, out,
    full_w, a_band, z_all, acc, ext, rim_send, rim_up, rim_down,
    edge_send, edge_recv, pol_send, pol, a_pol, z_pol,
    s1_send, s1_recv, s2_send, s2_recv, s3_send, s3_recv,
    rim_ss, rim_rs, edge_ss, edge_rs, p1_ss, p1_rs, p2_ss, p2_rs, own_sem,
):
    rows_dev, lon_dev, channels = signal.shape
    n_basis, c_dev, _ = mixing.shape
    support = sup_rows.shape[1]
    cycle = lon_dev * n_lon
    n_group = rows_dev // GROUP
    lat = lax.axis_index("lat")
    lon = lax.axis_index("lon")
    is_top = lat == 0
    is_bottom = lat == n_lat - 1
    is_polar = is_top | is_bottom
    sub = lat % PIECES
    lat_base = lat - sub
    peers = n_lon // 2
    partner = lon + 1 - 2 * (lon % 2)
    right = (lon + 1) % n_lon
    left = (lon + n_lon - 1) % n_lon
    ks = n_basis // CHUNKS

    live = band_rows[lat]
    first_row = 0
    for b in range(n_lat):
        first_row = first_row + jnp.where(b < lat, band_rows[b], 0)

    barrier = pltpu.get_barrier_semaphore()
    for d in range(1, peers):
        pl.semaphore_signal(barrier, inc=1, device_id=(lat, (lon + 2 * d) % n_lon), device_id_type=MESH)
    for e in range(1, PIECES):
        pl.semaphore_signal(barrier, inc=1, device_id=(lat_base + (sub + e) % PIECES, lon), device_id_type=MESH)
    pl.semaphore_signal(barrier, inc=1, device_id=(lat, right), device_id_type=MESH)
    pl.semaphore_signal(barrier, inc=1, device_id=(lat, left), device_id_type=MESH)

    @pl.when(lat > 0)
    def _():
        pl.semaphore_signal(barrier, inc=1, device_id=(lat - 1, lon), device_id_type=MESH)

    @pl.when(lat < n_lat - 1)
    def _():
        pl.semaphore_signal(barrier, inc=1, device_id=(lat + 1, lon), device_id_type=MESH)

    rim_send[...] = signal[pl.ds(jnp.clip(live - LAT_REACH, 0, rows_dev - LAT_REACH), LAT_REACH)]
    polar_start = jnp.where(is_bottom, jnp.clip(live - SPAN, 0, rows_dev - SPAN), 0)
    pol_rows = [signal[polar_start + r] for r in range(SPAN)]
    tail = jnp.zeros((POLAR_PAD - SPAN * lon_dev, channels), BF16)
    pol_send[...] = jnp.concatenate(pol_rows + [tail], axis=0)
    for r in range(rows_dev):
        edge_send[0, r] = signal[r, 0:LON_REACH]
        edge_send[1, r] = signal[r, lon_dev - LON_REACH : lon_dev]

    greeted = (peers - 1) + (PIECES - 1) + 2
    pl.semaphore_wait(barrier, greeted + jnp.where(lat > 0, 1, 0) + jnp.where(lat < n_lat - 1, 1, 0))

    def rows_of(source):
        return pl.ds(pl.multiple_of(source * c_dev, c_dev), c_dev)

    def lanes_of(piece):
        return pl.ds(pl.multiple_of(piece * 128, 128), 128)

    mine = rows_of(lon)
    q = lanes_of(sub)

    def stage1(d, j):
        kk = pl.ds(j * ks, ks)
        return rdma(
            mixing.at[kk, :, q], full_w.at[kk, mine, q], s1_send.at[d - 1, j], s1_recv.at[d - 1, j],
            lat, (lon + 2 * d) % n_lon,
        )

    def stage2(e, d, j):
        kk = pl.ds(j * ks, ks)
        region = full_w.at[kk, rows_of((lon + n_lon - 2 * d) % n_lon), q]
        return rdma(
            region, region, s2_send.at[e - 1, d - 1, j], s2_recv.at[e - 1, d - 1, j],
            lat_base + (sub + e) % PIECES, lon,
        )

    def stage3(d, j):
        kk = pl.ds(j * ks, ks)
        region = full_w.at[kk, rows_of((lon + n_lon - 2 * d) % n_lon), :]
        source = mixing.at[kk] if d == 0 else region
        return rdma(source, region, s3_send.at[d, j], s3_recv.at[d, j], lat, partner)

    up_copy = rdma(signal.at[pl.ds(0, LAT_REACH)], rim_down, rim_ss.at[0], rim_rs.at[0], lat - 1, lon)
    down_copy = rdma(rim_send, rim_up, rim_ss.at[1], rim_rs.at[1], lat + 1, lon)

    @pl.when(lat > 0)
    def _():
        up_copy.start()

    @pl.when(lat < n_lat - 1)
    def _():
        down_copy.start()

    for j in range(CHUNKS):
        for d in range(1, peers):
            stage1(d, j).start()
        stage3(0, j).start()
    own_copy = pltpu.make_async_copy(mixing, full_w.at[:, mine, :], own_sem)
    own_copy.start()

    def polar1(d):
        return rdma(pol_send, pol.at[lon, pl.ds(0, POLAR_PAD)], p1_ss.at[d - 1], p1_rs.at[d - 1], lat, (lon + 2 * d) % n_lon)

    def polar2(d):
        region = pol.at[(lon + n_lon - 2 * d) % n_lon, pl.ds(0, POLAR_PAD)]
        source = pol_send if d == 0 else region
        return rdma(source, region, p2_ss.at[d], p2_rs.at[d], lat, partner)

    @pl.when(is_top)
    def _():
        rim_up[...] = jnp.zeros_like(rim_up)

    @pl.when(is_bottom)
    def _():
        rim_down[...] = jnp.zeros_like(rim_down)

    @pl.when(is_polar)
    def _():
        for d in range(1, peers):
            polar1(d).start()
        polar2(0).start()
        pol[lon, pl.ds(0, POLAR_PAD)] = pol_send[...]
        for b in range(n_lon):
            pol[b, pl.ds(POLAR_PAD, 128 - POLAR_PAD)] = jnp.zeros((128 - POLAR_PAD, channels), BF16)

    col = lax.broadcasted_iota(jnp.int32, (PAD, 128), 1)
    pos = lax.broadcasted_iota(jnp.int32, (PAD, 128), 0)
    within = col % WIDE
    target = jnp.where(within < lon_dev, within, jnp.where(within < lon_dev + LON_REACH, within - lon_dev - LON_REACH, within - LON_REACH))
    code0 = jnp.where(within < lon_dev + 2 * LON_REACH, (col // WIDE) * 64 + target - pos + LON_REACH, -100000)
    half_rows = 128 // WIDE

    def accumulate(code, keys, grid_id):
        sums = [jnp.zeros((PAD, 128), F32) for _ in range(n_basis)]
        for s in range(support):
            hit = code == keys[s]
            for k in range(n_basis):
                sums[k] = sums[k] + jnp.where(hit, basis[grid_id, s * n_basis + k], 0.0)
        return sums

    def build_slot(i, carry):
        g = i // GROUP
        r = i % GROUP
        grid_id = jnp.minimum(first_row + i, grid_rows - 1)
        keys = []
        for s in range(support):
            off = sup_lons[grid_id, s]
            off = jnp.where(off > cycle // 2, off - cycle, off)
            window = sup_rows[grid_id, s] - first_row + LAT_REACH - g * GROUP
            keys.append(window * 64 + off + LON_REACH)
        for h in range(2):
            sums = accumulate(code0, [key - h * half_rows * 64 for key in keys], grid_id)
            for k in range(n_basis):
                a_band[g, k, pl.ds(pl.multiple_of(r * PAD, PAD), PAD), h * 128 : (h + 1) * 128] = sums[k]
        return carry

    def forward2(j):
        for d in range(1, peers):
            stage1(d, j).wait_recv()
            for e in range(1, PIECES):
                stage2(e, d, j).start()

    def forward3(j):
        for d in range(1, peers):
            for e in range(1, PIECES):
                stage2(e, d, j).wait_recv()
            stage3(d, j).start()

    lax.fori_loop(0, 4, build_slot, 0)

    @pl.when(lat > 0)
    def _():
        down_copy.wait_recv()

    @pl.when(lat < n_lat - 1)
    def _():
        up_copy.wait_recv()

    for r in range(LAT_REACH):
        edge_send[0, rows_dev + r] = rim_up[r, 0:LON_REACH]
        edge_send[1, rows_dev + r] = rim_up[r, lon_dev - LON_REACH : lon_dev]
        edge_send[0, rows_dev + LAT_REACH + r] = rim_down[r, 0:LON_REACH]
        edge_send[1, rows_dev + LAT_REACH + r] = rim_down[r, lon_dev - LON_REACH : lon_dev]
    lax.fori_loop(4, 6, build_slot, 0)
    to_left = rdma(edge_send.at[0], edge_recv.at[1], edge_ss.at[0], edge_rs.at[0], lat, left)
    to_right = rdma(edge_send.at[1], edge_recv.at[0], edge_ss.at[1], edge_rs.at[1], lat, right)
    to_left.start()
    to_right.start()
    forward2(0)
    lax.fori_loop(6, 14, build_slot, 0)
    forward2(1)
    lax.fori_loop(14, rows_dev, build_slot, 0)

    @pl.when(is_polar)
    def _():
        for d in range(1, peers):
            polar1(d).wait_recv()
            polar2(d).start()

    forward2(2)
    forward3(0)

    to_left.wait_recv()
    to_right.wait_recv()

    def source_row(slot, own, rim_u, rim_d):
        if slot < 0:
            return rim_u(slot + LAT_REACH)
        base = own(min(slot, rows_dev - 1))
        if slot < rows_dev // 2:
            return base
        value = jnp.where(live == slot, rim_d(0), base)
        return jnp.where(live + 1 == slot, rim_d(1), value)

    filler = jnp.zeros((WIDE - lon_dev - 2 * LON_REACH, channels), BF16)
    for e in range(rows_dev + 2 * LAT_REACH):
        centre = source_row(e - LAT_REACH, lambda r: signal[r], lambda r: rim_up[r], lambda r: rim_down[r])
        sides = [
            source_row(
                e - LAT_REACH,
                lambda r: edge_recv[side, r],
                lambda r: edge_recv[side, rows_dev + r],
                lambda r: edge_recv[side, rows_dev + LAT_REACH + r],
            )
            for side in range(2)
        ]
        ext[e] = jnp.concatenate([centre, sides[0], sides[1], filler], axis=0)

    out_base = jnp.where(is_bottom, grid_rows - POLAR_ROWS, 0)
    src_base = jnp.where(is_bottom, grid_rows - SPAN, 0)

    @pl.when(is_polar)
    def _():
        for d in range(peers):
            polar2(d).wait_recv()
        z_pol[...] = jnp.zeros_like(z_pol)
        prow = jnp.where(col >= lon_dev, 1, 0) + jnp.where(col >= 2 * lon_dev, 1, 0) + jnp.where(col >= 3 * lon_dev, 1, 0)
        pcol = col - prow * lon_dev

        def polar_block(b, carry):
            shift = pcol - pos + (b - lon) * lon_dev
            shift = jnp.where(shift < 0, shift + cycle, shift)
            code = jnp.where(col < SPAN * lon_dev, prow * cycle + shift, -100000)
            for r in range(POLAR_ROWS):
                grid_id = out_base + r
                keys = [(sup_rows[grid_id, s] - src_base) * cycle + sup_lons[grid_id, s] for s in range(support)]
                sums = accumulate(code, keys, grid_id)
                for k in range(n_basis):
                    a_pol[pl.ds((r * n_basis + k) * PAD, PAD), :] = sums[k]
            z_pol[...] += jnp.dot(a_pol[...].astype(BF16), pol[b], preferred_element_type=F32)
            return carry

        lax.fori_loop(0, n_lon, polar_block, 0)

    forward3(1)
    polar_slot = jnp.where(is_top, 0, jnp.where(is_bottom, live - POLAR_ROWS, -100))
    span_rows = GROUP * PAD
    group_slot = lax.broadcasted_iota(jnp.int32, (span_rows, channels), 0) // PAD

    def apply_group(g, carry):
        a_now = a_band[g].reshape(n_basis * span_rows, 256).astype(BF16)
        window = ext[pl.ds(g * GROUP, 2 * GROUP)].reshape(256, channels)
        terms = jnp.dot(a_now, window, preferred_element_type=F32)
        for k in range(n_basis):
            value = terms[k * span_rows : (k + 1) * span_rows]
            for r in range(POLAR_ROWS):
                chosen = z_pol[pl.ds((r * n_basis + k) * PAD, PAD), :]
                chosen = jnp.concatenate([chosen] * GROUP, axis=0)
                value = jnp.where(group_slot == polar_slot + r - g * GROUP, chosen, value)
            z_all[pl.ds(pl.multiple_of(g * span_rows, span_rows), span_rows), k * channels : (k + 1) * channels] = value.astype(BF16)
        return carry

    lax.fori_loop(0, n_group, apply_group, 0)
    forward3(2)

    own_copy.wait()
    half_m = rows_dev * PAD // 2
    acc[...] = jnp.zeros_like(acc)
    for j in range(CHUNKS):
        for d in range(peers):
            stage3(d, j).wait_recv()

        def mix(t, carry):
            k = j * ks + t // 2
            rows = pl.ds(pl.multiple_of((t % 2) * half_m, half_m), half_m)
            lhs = z_all[rows, pl.ds(pl.multiple_of(k * channels, channels), channels)]
            acc[rows, :] += jnp.dot(lhs, full_w[k], preferred_element_type=F32)
            return carry

        lax.fori_loop(0, 2 * ks, mix, 0)

    def put(i, carry):
        value = acc[pl.ds(pl.multiple_of(i * PAD, PAD), PAD), :]
        value = jnp.where(i < live, value, 0.0)
        out[i] = value[0:lon_dev].astype(BF16)
        return carry

    lax.fori_loop(0, rows_dev, put, 0)

    to_left.wait_send()
    to_right.wait_send()

    @pl.when(lat > 0)
    def _():
        up_copy.wait_send()

    @pl.when(lat < n_lat - 1)
    def _():
        down_copy.wait_send()

    @pl.when(is_polar)
    def _():
        for d in range(peers):
            if d:
                polar1(d).wait_send()
            polar2(d).wait_send()

    for j in range(CHUNKS):
        for d in range(peers):
            stage3(d, j).wait_send()
            if d:
                stage1(d, j).wait_send()
                for e in range(1, PIECES):
                    stage2(e, d, j).wait_send()


def solution(mesh):
    n_lat, n_lon = mesh.shape["lat"], mesh.shape["lon"]

    def per_device(signal, band_rows, support_rows, support_lons, basis_values, mixing):
        rows_dev, lon_dev, channels = signal.shape
        n_basis, c_dev, outs = mixing.shape
        grid_rows, support = support_rows.shape
        peers = n_lon // 2
        table = basis_values.astype(F32).reshape(grid_rows, support * n_basis)
        vmem = pl.BlockSpec(memory_space=pltpu.VMEM)
        smem = pl.BlockSpec(memory_space=pltpu.SMEM)
        dma = pltpu.SemaphoreType.DMA
        return pl.pallas_call(
            functools.partial(kernel, n_lat, n_lon, grid_rows),
            out_shape=jax.ShapeDtypeStruct((rows_dev, lon_dev, outs), BF16),
            in_specs=[vmem, smem, smem, smem, smem, vmem],
            out_specs=vmem,
            scratch_shapes=[
                pltpu.VMEM((n_basis, n_lon * c_dev, outs), BF16),
                pltpu.VMEM((rows_dev // GROUP, n_basis, GROUP * PAD, 256), F32),
                pltpu.VMEM((rows_dev * PAD, n_basis * channels), BF16),
                pltpu.VMEM((rows_dev * PAD, outs), F32),
                pltpu.VMEM((rows_dev + 2 * LAT_REACH, WIDE, channels), BF16),
                pltpu.VMEM((LAT_REACH, lon_dev, channels), BF16),
                pltpu.VMEM((LAT_REACH, lon_dev, channels), BF16),
                pltpu.VMEM((LAT_REACH, lon_dev, channels), BF16),
                pltpu.VMEM((2, rows_dev + 2 * LAT_REACH, LON_REACH, channels), BF16),
                pltpu.VMEM((2, rows_dev + 2 * LAT_REACH, LON_REACH, channels), BF16),
                pltpu.VMEM((POLAR_PAD, channels), BF16),
                pltpu.VMEM((n_lon, 128, channels), BF16),
                pltpu.VMEM((POLAR_ROWS * n_basis * PAD, 128), F32),
                pltpu.VMEM((POLAR_ROWS * n_basis * PAD, channels), F32),
                dma((peers - 1, CHUNKS)), dma((peers - 1, CHUNKS)),
                dma((PIECES - 1, peers - 1, CHUNKS)), dma((PIECES - 1, peers - 1, CHUNKS)),
                dma((peers, CHUNKS)), dma((peers, CHUNKS)),
                dma((2,)), dma((2,)), dma((2,)), dma((2,)),
                dma((peers - 1,)), dma((peers - 1,)), dma((peers,)), dma((peers,)), dma(()),
            ],
            compiler_params=pltpu.CompilerParams(
                collective_id=0, has_side_effects=True, vmem_limit_bytes=60 * 1024 * 1024
            ),
        )(signal, band_rows, support_rows, support_lons, table, mixing)

    placed = (P("lat", "lon", None), P(), P(), P(), P(), P(None, "lon", None))
    return jax.shard_map(
        per_device, mesh=mesh, in_specs=placed, out_specs=P("lat", "lon", None), check_vma=False
    )
```

time: 171 us -> 51.6 us (0.30)
  local copies, waits for them, and re-layouts: 85 us -> 5.81 us
  Pallas kernels: 0 us -> 45.5 us
  blocking collectives: 18.6 us -> 0 us
  matrix products: 17.3 us -> 0 us
  between operations: 16.7 us -> 0.03 us
  waiting for transfers between devices: 13.6 us -> 0 us
  starting transfers between devices: 9.7 us -> 0 us
  other arithmetic: 6.76 us -> 0 us
  loops' own time: 2.05 us -> 0 us
    gather x23 -> x0, local copies, waits for them, and re-layouts: 54.7 us -> none  [the longest x6 32.3 us: band_piece(): lax.dynamic_slice(cycle_cells, (row_id, col_id, 0), (1, lon_dev, channels))]
    pallas_call x0 -> x1, Pallas kernels: none -> 45.5 us  [per_device(): pl.pallas_call(functools.partial(kernel, n_lat, n_lon, grid_rows), out_sh...]
    all_gather x1 -> x0, blocking collectives: 18.6 us -> none  [per_device(): whole_cycle = lax.all_gather(polar_source, 'lon', axis=1, tiled=True)]
    dot_general x7 -> x0, matrix products: 17.3 us -> none  [the longest x3 12.4 us: block_out(): jnp.einsum('rklc,kco->rlo', basis_terms, full_mixing, preferred_element_t...]
    all_gather x1 -> x0, waiting for transfers between devices: 11 us -> none  [per_device(): full_mixing = lax.all_gather(mixing, 'lon', axis=1, tiled=True)]
    squeeze x4 -> x0, local copies, waits for them, and re-layouts: 10.3 us -> none  [contract_rows(): flattened = pieces.reshape(pieces.shape[0], -1)]
    ppermute x4 -> x0, starting transfers between devices: 9.7 us -> none  [the longest x2 5.21 us: extended_2(): lax.ppermute(lax.slice_in_dim(block, block.shape[dim] - width, None, axis...]
    convert_element_type x3 -> x0, local copies, waits for them, and re-layouts: 5.7 us -> none  [contract_rows(): summed.astype(jnp.bfloat16)]
  transfers between devices with their start and end apart: 5 -> 0, of which waited for: 2 -> 0; matrix products, arithmetic and copies ran while one was open for 10% -> 0% of each run, Pallas kernels for 0% -> 0%
where the time goes in v1:
time: 51.6 us; the launch traced here: 51.4 us
  Pallas kernels  45.5 us (88%)
  local copies, waits for them, and re-layouts  5.81 us (11%)
    pallas_call x1, Pallas kernels, per_device(): pl.pallas_call(functools.partial(kernel, n_lat, n_lon, grid_rows), out_sh...  45.5 us
    unnamed x9, local copies, waits for them, and re-layouts  3.11 us
    pallas_call x1, local copies, waits for them, and re-layouts, per_device(): pl.pallas_call(functools.partial(kernel, n_lat, n_lon, grid_rows), out_sh...  1.96 us

profile of v1, /device:TPU:0, one launch (start us, length us, event | category | flops | bytes accessed | tf_op | source)
XLA Modules:
  0.0 51.4 jit_solution(14193349430348228768)
XLA Ops:
  0.0 0.0 copy-start.1
  0.0 0.0 copy-start.2
  0.0 0.0 copy-start
  0.0 1.5 %copy.14.sup_rows = s32[72,16]{1,0:T(8,128)} copy(s32[72,16]{0,1:T(8,128)} %param.8) | data formatting | bytes 9216 | tf_op args[2]
  1.5 0.0 copy-done.2
  1.5 0.7 %copy.15.sup_lons = s32[72,16]{1,0:T(8,128)} copy(s32[72,16]{0,1:T(8,128)S(1)} %copy-done.2) | data formatting | bytes 9216 | tf_op args[3]
  2.2 0.0 copy-done.1
  2.2 0.7 %copy.16.basis = f32[72,144]{1,0:T(8,128)} copy(f32[72,144]{0,1:T(8,128)S(1)} %reshape.8) | data formatting | bytes 82944 | tf_op jit(solution)/shard_map/reshape | solution.py:373
  2.9 0.0 copy-done
  2.9 0.9 %copy.13.signal = bf16[24,18,512]{2,1,0:T(8,128)(2,1)} copy(bf16[24,18,512]{2,0,1:T(8,128)(2,1)S(1)} %copy-done) | data formatting | bytes 884736 | tf_op args[0]
  3.9 45.5 %shard_map.64 = bf16[24,18,512]{2,1,0:T(8,128)(2,1)} custom-call(bf16[24,18,512]{2,1,0:T(8,128)(2,1)} %copy.13.signal, s32[4]{0:T(128)} %band_rows.1, s32[72,16]{1,0:T(8,128)} %copy.14.sup_rows, s32[72,16]{1,0:T(8,128)} %copy.15.sup_lons, f32[72,144]{1,0:T(8,128)} %copy.16.basis, bf16[9,64,512]{2,1,0:T(8,128)(2,1)} %mixing.1), custom_call_target="tpu_custom_call" | custom-call | tf_op jit(solution)/shard_map/pallas_call | solution.py:377
  49.4 2.0 %copy.17 = bf16[24,18,512]{2,0,1:T(8,128)(2,1)} copy(bf16[24,18,512]{2,1,0:T(8,128)(2,1)} %shard_map.64) | data formatting | bytes 884736 | tf_op jit(solution)/shard_map/pallas_call | solution.py:377
  (2 shorter events, 0.0 us)
Async XLA Ops:
  0.0 2.2 %copy-start.1 = (bf16[72,16,9]{0,1,2:T(8,128)(2,1)S(1)}, bf16[72,16,9]{0,1,2:T(8,128)(2,1)}, u32[]{:S(2)}) copy-start(bf16[72,16,9]{0,1,2:T(8,128)(2,1)} %param.10) | copy-start | bytes 62212
  0.0 1.5 %copy-start.2 = (s32[72,16]{0,1:T(8,128)S(1)}, s32[72,16]{0,1:T(8,128)}, u32[]{:S(2)}) copy-start(s32[72,16]{0,1:T(8,128)} %param.9) | copy-start | bytes 13828
  0.0 2.9 %copy-start = (bf16[24,18,512]{2,0,1:T(8,128)(2,1)S(1)}, bf16[24,18,512]{2,0,1:T(8,128)(2,1)}, u32[]{:S(2)}) copy-start(bf16[24,18,512]{2,0,1:T(8,128)(2,1)} %param.6) | copy-start | bytes 1327108

commit v2 on v1

--- a/solution.py
+++ b/solution.py
@@ -39,7 +39,7 @@
 ):
     rows_dev, lon_dev, channels = signal.shape
     n_basis, c_dev, _ = mixing.shape
-    support = sup_rows.shape[1]
+    support = sup_rows.shape[0]
     cycle = lon_dev * n_lon
     n_group = rows_dev // GROUP
     lat = lax.axis_index("lat")
@@ -173,7 +173,7 @@
         for s in range(support):
             hit = code == keys[s]
             for k in range(n_basis):
-                sums[k] = sums[k] + jnp.where(hit, basis[grid_id, s * n_basis + k], 0.0)
+                sums[k] = sums[k] + jnp.where(hit, basis[k * support + s, grid_id], 0.0)
         return sums
 
     def build_slot(i, carry):
@@ -182,9 +182,9 @@
         grid_id = jnp.minimum(first_row + i, grid_rows - 1)
         keys = []
         for s in range(support):
-            off = sup_lons[grid_id, s]
+            off = sup_lons[s, grid_id]
             off = jnp.where(off > cycle // 2, off - cycle, off)
-            window = sup_rows[grid_id, s] - first_row + LAT_REACH - g * GROUP
+            window = sup_rows[s, grid_id] - first_row + LAT_REACH - g * GROUP
             keys.append(window * 64 + off + LON_REACH)
         for h in range(2):
             sums = accumulate(code0, [key - h * half_rows * 64 for key in keys], grid_id)
@@ -281,7 +281,7 @@
             code = jnp.where(col < SPAN * lon_dev, prow * cycle + shift, -100000)
             for r in range(POLAR_ROWS):
                 grid_id = out_base + r
-                keys = [(sup_rows[grid_id, s] - src_base) * cycle + sup_lons[grid_id, s] for s in range(support)]
+                keys = [(sup_rows[s, grid_id] - src_base) * cycle + sup_lons[s, grid_id] for s in range(support)]
                 sums = accumulate(code, keys, grid_id)
                 for k in range(n_basis):
                     a_pol[pl.ds((r * n_basis + k) * PAD, PAD), :] = sums[k]
@@ -370,7 +370,7 @@
         n_basis, c_dev, outs = mixing.shape
         grid_rows, support = support_rows.shape
         peers = n_lon // 2
-        table = basis_values.astype(F32).reshape(grid_rows, support * n_basis)
+        table = jnp.transpose(basis_values, (2, 1, 0)).astype(F32).reshape(n_basis * support, grid_rows)
         vmem = pl.BlockSpec(memory_space=pltpu.VMEM)
         smem = pl.BlockSpec(memory_space=pltpu.SMEM)
         dma = pltpu.SemaphoreType.DMA
@@ -403,7 +403,7 @@
             compiler_params=pltpu.CompilerParams(
                 collective_id=0, has_side_effects=True, vmem_limit_bytes=60 * 1024 * 1024
             ),
-        )(signal, band_rows, support_rows, support_lons, table, mixing)
+        )(signal, band_rows, support_rows.T, support_lons.T, table, mixing)
 
     placed = (P("lat", "lon", None), P(), P(), P(), P(), P(None, "lon", None))
     return jax.shard_map(

time: 51.6 us -> 50.2 us (0.973)
  local copies, waits for them, and re-layouts: 5.81 us -> 3.92 us
  other arithmetic: 0 us -> 1.41 us
  Pallas kernels: 45.5 us -> 44.6 us
    reshape x0 -> x1, other arithmetic: none -> 1.41 us  [per_device(): jnp.transpose(basis_values, (2, 1, 0)).astype(F32)]
    unnamed x9 -> x1, local copies, waits for them, and re-layouts: 3.11 us -> 1.96 us
    pallas_call x1, Pallas kernels: 45.5 us -> 44.6 us  [per_device(): pl.pallas_call(functools.partial(kernel, n_lat, n_lon, grid_rows), out_sh...]
    reshape x3 -> x0, local copies, waits for them, and re-layouts: 0.74 us -> none  [per_device(): table = basis_values.astype(F32).reshape(grid_rows, support * n_basis)]
where the time goes in v2:
time: 50.2 us; the launch traced here: 49.9 us
  Pallas kernels  44.6 us (89%)
  local copies, waits for them, and re-layouts  3.92 us (8%)
  other arithmetic  1.41 us (3%)
    pallas_call x1, Pallas kernels, per_device(): pl.pallas_call(functools.partial(kernel, n_lat, n_lon, grid_rows), out_sh...  44.6 us
    pallas_call x1, local copies, waits for them, and re-layouts, per_device(): pl.pallas_call(functools.partial(kernel, n_lat, n_lon, grid_rows), out_sh...  1.96 us
    unnamed x1, local copies, waits for them, and re-layouts  1.96 us
    reshape x1, other arithmetic, per_device(): jnp.transpose(basis_values, (2, 1, 0)).astype(F32)  1.41 us

profile of v2, /device:TPU:0, one launch (start us, length us, event | category | flops | bytes accessed | tf_op | source)
XLA Modules:
  0.0 49.9 jit_solution(4996873847303250290)
XLA Ops:
  0.0 1.4 %reshape.9 = f32[72,16,9]{0,1,2:T(8,128)} convert(bf16[72,16,9]{0,1,2:T(8,128)(2,1)} %param.10) | non-fusion elementwise | flops 10368 | bytes 62208 | tf_op jit(solution)/shard_map/reshape | solution.py:373
  1.4 2.0 %copy.7.signal = bf16[24,18,512]{2,1,0:T(8,128)(2,1)} copy(bf16[24,18,512]{2,0,1:T(8,128)(2,1)} %param.6) | data formatting | bytes 884736 | tf_op args[0]
  3.4 44.6 %shard_map.64 = bf16[24,18,512]{2,1,0:T(8,128)(2,1)} custom-call(bf16[24,18,512]{2,1,0:T(8,128)(2,1)} %copy.7.signal, s32[4]{0:T(128)} %band_rows.1, s32[16,72]{1,0:T(8,128)} %bitcast.6, s32[16,72]{1,0:T(8,128)} %bitcast.7, f32[144,72]{1,0:T(8,128)} %bitcast.5, bf16[9,64,512]{2,1,0:T(8,128)(2,1)} %mixing.1), custom_call_target="tpu_custom_call" | custom-call | tf_op jit(solution)/shard_map/pallas_call | solution.py:377
  47.9 2.0 %copy.8 = bf16[24,18,512]{2,0,1:T(8,128)(2,1)} copy(bf16[24,18,512]{2,1,0:T(8,128)(2,1)} %shard_map.64) | data formatting | bytes 884736 | tf_op jit(solution)/shard_map/pallas_call | solution.py:377
